TPU v7x, 32 devices: a whole 2x2x4 slice. The times are simulated.
32 devices in a mesh: role: 4 (over y, core), shard: 8 (over z, x).
Axes of the slice: x: 2, y: 2, z: 4, core: 2. Of those that a mesh axis runs over, the one named last changes fastest.
Arguments:
- gradient: bfloat16 [2560, 2560], P('shard', 'role'), may hold values from -1200 to 1200
- left_old: float32 [2560, 2560], P('shard', 'role'), may hold values from -1 to 10, as said below
- right_old: float32 [2560, 2560], P('shard', 'role'), may hold values from -1 to 10, as said below
- basis_old: bfloat16 [2560, 512], P('shard', 'role'), may hold values from -1 to 1
Outputs:
- left_stat: float32 [2560, 2560], P('shard', 'role')
- right_stat: float32 [2560, 2560], P('shard', 'role')
- left_basis: float32 [2560, 512], P('shard', 'role')
Inputs may be any that keep to these rules, and one draw needn't show every extreme that they name: `left_old`: symmetric and positive definite. `right_old`: symmetric and positive definite.
All inputs are finite; a program needn't handle non-finite values.
Results may differ from a plain program's by a relative error of at most 0.0003.
Values may be sent and summed in bfloat16 or wider, within the bound.
No kernel may reach another device: no remote copies, remote signals or barrier semaphores. Data moves between devices by JAX's collectives and lax.ppermute only.
A program may use at most 64 MiB of HBM per device.

v0:
```python
import jax
import jax.numpy as jnp
from jax import lax
from jax.sharding import PartitionSpec as P

smoothing = 0.95
clip_ratio = 4.0
epsilon_value = 1e-06


def lower_gram(power_row, role_count, role_at):
    order_size = power_row.shape[1]
    tile_size = order_size // (2 * role_count)
    second_row = 2 * role_count - 1 - role_at

    def strip(tile_row):
        chosen = lax.dynamic_slice_in_dim(power_row, tile_row * tile_size, tile_size, 1)
        return lax.dot_general(
            chosen,
            power_row,
            (((0,), (0,)), ((), ())),
            precision=lax.Precision.HIGHEST,
            preferred_element_type=jnp.float32,
        )

    strip_first = strip(role_at)
    strip_second = strip(second_row)
    split_at = (role_at + 1) * tile_size
    packed_width = order_size + tile_size
    first_ext = jnp.concatenate(
        [strip_first, jnp.zeros((tile_size, tile_size), jnp.float32)], axis=1
    )
    padded_second = jnp.concatenate(
        [jnp.zeros((tile_size, order_size), jnp.float32), strip_second], axis=1
    )
    second_ext = lax.dynamic_slice_in_dim(padded_second, order_size - split_at, packed_width, 1)
    columns = lax.broadcasted_iota(jnp.int32, (tile_size, packed_width), 1)
    packed = jnp.where(columns < split_at, first_ext, second_ext)
    tile_sums = lax.psum(packed, "shard")
    strips = lax.all_gather(tile_sums, "role", axis=0, tiled=True)
    lower_part = jnp.zeros((order_size, order_size), jnp.float32)
    for member in range(role_count):
        packed_row = strips[member * tile_size : (member + 1) * tile_size]
        head = (member + 1) * tile_size
        other = 2 * role_count - 1 - member
        tail = (2 * role_count - member) * tile_size
        lower_part = lower_part.at[member * tile_size : head, :head].set(packed_row[:, :head])
        lower_part = lower_part.at[other * tile_size : (other + 1) * tile_size, :tail].set(
            packed_row[:, head : head + tail]
        )
    return jnp.tril(lower_part) + jnp.transpose(jnp.tril(lower_part, -1))


def on_device(gradient, left_old, right_old, basis_old):
    row_count, col_count = gradient.shape
    vec_count = basis_old.shape[1]
    order_size = row_count * lax.axis_size("shard")
    role_count = lax.axis_size("role")
    role_at = lax.axis_index("role")
    col_start = role_at * col_count
    vec_start = role_at * vec_count
    gradient_wide = gradient.astype(jnp.float32)
    squares = lax.psum(jnp.sum(gradient_wide * gradient_wide), ("role", "shard"))
    factor = jnp.minimum(
        1.0, clip_ratio * jnp.sqrt(jnp.float32(order_size)) / jnp.sqrt(squares + epsilon_value)
    )
    squared = factor * factor
    grad_row = lax.all_gather(gradient, "role", axis=1, tiled=True)
    left_part = lax.dot_general(
        gradient,
        lax.all_gather(gradient, "shard", axis=0, tiled=True),
        (((1,), (1,)), ((), ())),
        preferred_element_type=jnp.float32,
    )
    right_share = lax.psum_scatter(
        lax.dot_general(
            grad_row, gradient, (((0,), (0,)), ((), ())), preferred_element_type=jnp.float32
        ),
        "shard",
        scatter_dimension=0,
        tiled=True,
    )
    placed = lax.dynamic_update_slice_in_dim(
        jnp.zeros((row_count, order_size), jnp.float32), left_old, col_start, 1
    )
    left_row = lax.psum((1.0 - smoothing) * squared * left_part + smoothing * placed, "role")
    left_stat = lax.dynamic_slice_in_dim(left_row, col_start, col_count, 1)
    right_stat = smoothing * right_old + (1.0 - smoothing) * squared * right_share
    power_block = jnp.dot(
        left_row,
        lax.all_gather(basis_old, "shard", axis=0, tiled=True).astype(jnp.float32),
        precision=lax.Precision.HIGHEST,
    )
    power_row = lax.all_gather(power_block, "role", axis=1, tiled=True)
    gram_full = lower_gram(power_row, role_count, role_at)
    factor_lower = jnp.linalg.cholesky(gram_full)
    solved = jax.scipy.linalg.solve_triangular(factor_lower, power_row.T, lower=True)
    left_basis = lax.dynamic_slice_in_dim(solved, vec_start, vec_count, 0).T
    return (left_stat, right_stat, left_basis)


def solution(mesh):
    return jax.shard_map(
        on_device,
        mesh=mesh,
        in_specs=(P("shard", "role"), P("shard", "role"), P("shard", "role"), P("shard", "role")),
        out_specs=(P("shard", "role"), P("shard", "role"), P("shard", "role")),
        check_vma=False,
    )
```

profile of v0, /device:TPU:0, one launch (start us, length us, event | category | flops | bytes accessed | tf_op | source)
XLA Modules:
  0.0 411.2 jit_solution(2077507508806869421)
XLA Ops:
  7.9 1.8 multiply_reduce_fusion
  9.8 44.0 %psum.21 = f32[]{:T(128)} all-reduce(f32[]{:T(128)} %multiply_reduce_fusion), channel_id=1, replica_groups=mesh['role'=4,'shard'=8] {'role','shard'}, use_global_device_ids=true, to_apply=%region_1.0 | all-reduce | flops 1 | bytes 8 | tf_op jit(solution)/shard_map/psum | solution.py:63
  55.7 20.1 %all-gather.3.cloned.1.call-done = bf16[2560,640]{1,0:T(8,128)(2,1)} async-done(((bf16[320,640]{1,0:T(8,128)(2,1)}), bf16[2560,640]{1,0:T(8,128)(2,1)}) %all-gather.3.cloned.1.call-update) | async-done | bytes 3276816 | tf_op jit(solution)/shard_map/all_gather | solution.py:71
  75.8 5.2 %fusion = f32[320,2560]{1,0:T(8,128)} fusion(bf16[320,640]{1,0:T(8,128)(2,1)} %param.20, bf16[2560,640]{1,0:T(8,128)(2,1)} %all-gather.3.cloned.1.call-done, f32[320,2560]{1,0:T(8,128)S(1)} %constant_dynamic-update-slice_fusion.1, f32[]{:T(128)S(6)} %mul.51), kind=kOutput, calls=%fused_computation.3 | convolution fusion | flops 1051033600 | bytes 10240004 | tf_op jit(solution)/shard_map/dot_general | solution.py:69
  81.9 31.9 %all_gather.17 = bf16[2560,128]{1,0:T(8,128)(2,1)S(1)} all-gather(bf16[320,128]{1,0:T(8,128)(2,1)S(1)} %copy-done.3), channel_id=1, replica_groups=mesh['role'=4,'shard'=8] {'shard'}, dimensions={0}, use_global_device_ids=true | all-gather | bytes 737280 | tf_op jit(solution)/shard_map/all_gather | solution.py:91
  113.8 36.7 %all-reduce.7.cloned.1.call-done = f32[320,2560]{1,0:T(8,128)} async-done(((f32[320,2560]{1,0:T(8,128)}), f32[320,2560]{1,0:T(8,128)}) %all-reduce.7.cloned.1.call-update) | async-done | bytes 3276816 | tf_op jit(solution)/shard_map/psum | solution.py:86
  150.5 3.5 fusion.45
  154.0 7.2 %all_gather.18 = f32[320,512]{1,0:T(8,128)S(1)} all-gather(f32[320,128]{1,0:T(8,128)S(1)} %fusion.45), channel_id=1, replica_groups=mesh['role'=4,'shard'=8] {'role'}, dimensions={1}, use_global_device_ids=true | all-gather | bytes 819200 | tf_op jit(solution)/shard_map/all_gather | solution.py:94
  163.3 8.9 %all-gather.5.cloned.1.call-done = bf16[320,2560]{1,0:T(8,128)(2,1)} async-done(((bf16[320,640]{1,0:T(8,128)(2,1)}), bf16[320,2560]{1,0:T(8,128)(2,1)}) %all-gather.5.cloned.1.call-update) | async-done | bytes 1638416 | tf_op jit(solution)/shard_map/all_gather | solution.py:68
  172.2 6.3 %fusion.44 = f32[2560,640]{1,0:T(8,128)} fusion(bf16[320,2560]{1,0:T(8,128)(2,1)} %all-gather.5.cloned.1.call-done, bf16[320,640]{1,0:T(8,128)(2,1)S(1)} %copy-done), kind=kOutput, calls=%fused_computation.97 | convolution fusion | flops 1048576000 | bytes 8601600 | tf_op jit(solution)/shard_map/dot_general | solution.py:76
  178.5 2.1 constant_dynamic-slice_fusion.1
  180.6 65.4 %all-reduce.9.cloned.1.call-done = f32[64,576]{1,0:T(8,128)} async-done(((f32[64,576]{1,0:T(8,128)}), f32[64,576]{1,0:T(8,128)}) %all-reduce.9.cloned.1.call-update) | async-done | bytes 147472 | tf_op jit(solution)/shard_map/psum | solution.py:39
  246.0 8.1 %all_gather.19 = f32[256,576]{1,0:T(8,128)S(1)} all-gather(f32[64,576]{1,0:T(8,128)} %all-reduce.9.cloned.1.call-done), channel_id=1, replica_groups=mesh['role'=4,'shard'=8] {'role'}, dimensions={0}, use_global_device_ids=true | all-gather | bytes 737280 | tf_op jit(solution)/shard_map/all_gather | solution.py:40
  257.8 2.1 scatter.39
  264.4 11.7 %cholesky.103 = f32[128,128]{1,0:T(8,128)S(1)} custom-call(f32[128,128]{1,0:T(8,128)S(1)} %cholesky.263), custom_call_target="Cholesky" | custom-call | tf_op jit(solution)/shard_map/jit(cholesky)/cholesky | solution.py:96
  276.2 9.8 %custom-call.31 = f32[1,128,128]{1,2,0:T(8,128)S(1)} custom-call(f32[1,128,128]{2,1,0:T(8,128)S(1)} %get-tuple-element.126), custom_call_target="InvertDiagBlocksLowerTriangular" | custom-call | tf_op jit(solution)/shard_map/jit(cholesky)/cholesky | solution.py:96
  288.6 11.7 %cholesky.215 = f32[128,128]{1,0:T(8,128)S(1)} custom-call(f32[128,128]{1,0:T(8,128)S(1)} %cholesky.267), custom_call_target="Cholesky" | custom-call | tf_op jit(solution)/shard_map/jit(cholesky)/cholesky | solution.py:96
  300.4 10.0 %custom-call.32 = f32[1,128,128]{1,2,0:T(8,128)S(1)} custom-call(f32[1,128,128]{2,1,0:T(8,128)S(1)} %get-tuple-element.123), custom_call_target="InvertDiagBlocksLowerTriangular" | custom-call | tf_op jit(solution)/shard_map/jit(cholesky)/cholesky | solution.py:96
  311.9 11.7 %cholesky.236 = f32[128,128]{1,0:T(8,128)S(1)} custom-call(f32[128,128]{1,0:T(8,128)S(1)} %cholesky.272), custom_call_target="Cholesky" | custom-call | tf_op jit(solution)/shard_map/jit(cholesky)/cholesky | solution.py:96
  323.6 9.8 %custom-call.33 = f32[1,128,128]{1,2,0:T(8,128)S(1)} custom-call(f32[1,128,128]{2,1,0:T(8,128)S(1)} %get-tuple-element.120), custom_call_target="InvertDiagBlocksLowerTriangular" | custom-call | tf_op jit(solution)/shard_map/jit(cholesky)/cholesky | solution.py:96
  334.9 11.9 %cholesky.253 = f32[128,128]{1,0:T(8,128)S(1)} custom-call(f32[128,128]{1,0:T(8,128)S(1)} %convolution_subtract_fusion.5), custom_call_target="Cholesky" | custom-call | tf_op jit(solution)/shard_map/jit(cholesky)/cholesky | solution.py:96
  351.5 8.0 %while.9 = (s32[]{:T(128)}, f32[512,512]{1,0:T(8,128)S(1)}, s32[4,2]{0,1:T(2,128)S(1)}, f32[4,128,128]{2,1,0:T(8,128)S(1)}, s32[]{:T(128)}) while((s32[]{:T(128)}, f32[512,512]{1,0:T(8,128)S(1)}, s32[4,2]{0,1:T(2,128)S(1)}, f32[4,128,128]{2,1,0:T(8,128)S(1)}, s32[]{:T(128)}) %tuple.63), condition=%wide.while_cond.8, body=%wide.while_body.8.sunk | while | flops 2 | bytes 131181 | solution.py:97
  359.6 39.3 %custom-call.34 = f32[4,128,128]{1,2,0:T(8,128)S(1)} custom-call(f32[4,128,128]{2,1,0:T(8,128)S(1)} %get-tuple-element.106), custom_call_target="InvertDiagBlocksLowerTriangular" | custom-call | tf_op jit(solution)/shard_map/jit(_solve_triangular)/triangular_solve | solution.py:97
  402.1 2.4 multiply_add_fusion
  (83 shorter events, 31.9 us)
Async XLA Ops:
  7.2 68.6 %all-gather.3.cloned.1.call-start = ((), (), s32[]{:S(2)}) async-start(), calls=%async_computation.1 | async-start | bytes 3686400 | tf_op jit(solution)/shard_map/all_gather | solution.py:71
  7.9 142.6 %all-reduce.7.cloned.1.call-start = ((), (), s32[]{:S(2)}) async-start(), calls=%async_computation.2 | async-start | bytes 6553600 | tf_op jit(solution)/shard_map/psum | solution.py:86
  54.4 1.1 copy-start.2
  81.0 0.9 copy-start.3
  81.0 91.2 %all-gather.5.cloned.1.call-start = ((), (), s32[]{:S(2)}) async-start(), calls=%async_computation.3 | async-start | bytes 2048000 | tf_op jit(solution)/shard_map/all_gather | solution.py:68
  81.8 164.2 %all-reduce.9.cloned.1.call-start = ((), (), s32[]{:S(2)}) async-start(), calls=%async_computation.5 | async-start | bytes 327680 | tf_op jit(solution)/shard_map/psum | solution.py:39
  113.8 58.4 %copy-start = (bf16[320,640]{1,0:T(8,128)(2,1)S(1)}, bf16[320,640]{1,0:T(8,128)(2,1)}, u32[]{:S(2)}) copy-start(bf16[320,640]{1,0:T(8,128)(2,1)} %param.20) | copy-start | bytes 1228804
  163.3 238.8 %reduce-scatter.2.cloned.1.call-start = ((), (), s32[]{:S(2)}) async-start(), calls=%async_computation.4 | async-start | bytes 7372800 | tf_op jit(solution)/shard_map/reduce_scatter | solution.py:75
  263.4 1.0 copy-start.1
Sparse Core Ops, SparseCore 0:
  10.2 65.5 all-gather.2
  81.1 69.3 all-reduce.6
  152.1 20.0 all-gather.4
  176.0 69.9 all-reduce.8
  249.5 121.9 reduce-scatter.1
where the time goes:
time: 419 us; the launch traced here: 411 us
  waiting for transfers between devices  132 us (32%)
  other arithmetic  126 us (30%)
  blocking collectives  91.2 us (22%)
  matrix products  24.1 us (6%)
  local copies, waits for them, and re-layouts  19.9 us (5%)
  between operations  17.7 us (4%)
    another operation x14, other arithmetic, on_device(): factor_lower = jnp.linalg.cholesky(gram_full)  78.7 us
    psum x1, waiting for transfers between devices, lower_gram(): tile_sums = lax.psum(packed, 'shard')  65.4 us
    psum x1, blocking collectives, on_device(): lax.psum(jnp.sum(gradient_wide * gradient_wide), ('role', 'shard'))  44 us
    another operation x3, other arithmetic, on_device(): jax.scipy.linalg.solve_triangular(factor_lower, power_row.T, lower=True)  39.4 us
    psum x1, waiting for transfers between devices, on_device(): lax.psum((1.0 - smoothing) * squared * left_part + smoothing * placed, 'r...  36.7 us
    all_gather x1, blocking collectives, on_device(): lax.all_gather(basis_old, 'shard', axis=0, tiled=True).astype(jnp.float32)  31.9 us
    all_gather x1, waiting for transfers between devices, on_device(): lax.all_gather(gradient, 'shard', axis=0, tiled=True)  20.1 us
    all_gather x1, waiting for transfers between devices, on_device(): grad_row = lax.all_gather(gradient, 'role', axis=1, tiled=True)  8.91 us
  transfers between devices with their start and end apart: 5, of which 4 were waited for; matrix products, arithmetic and copies ran while one was open for 39% of the time, Pallas kernels for 0%

commit v1 on v0

--- a/solution.py
+++ b/solution.py
@@ -36,7 +36,11 @@
     second_ext = lax.dynamic_slice_in_dim(padded_second, order_size - split_at, packed_width, 1)
     columns = lax.broadcasted_iota(jnp.int32, (tile_size, packed_width), 1)
     packed = jnp.where(columns < split_at, first_ext, second_ext)
-    tile_sums = lax.psum(packed, "shard")
+    tile_sums = packed
+    for hop in (1, 2, 4):
+        tile_sums = tile_sums + lax.ppermute(
+            tile_sums, "shard", [(dev, dev ^ hop) for dev in range(8)]
+        )
     strips = lax.all_gather(tile_sums, "role", axis=0, tiled=True)
     lower_part = jnp.zeros((order_size, order_size), jnp.float32)
     for member in range(role_count):

time: 419 us -> 402 us (0.959)
  waiting for transfers between devices: 132 us -> 111 us
    psum x1 -> x0, waiting for transfers between devices: 65.4 us -> none  [lower_gram(): tile_sums = lax.psum(packed, 'shard')]
    ppermute x0 -> x3, waiting for transfers between devices: none -> 42.2 us  [lower_gram(): lax.ppermute(tile_sums, 'shard', [(dev, dev ^ hop) for dev in range(8)])]
    all_gather x1, waiting for transfers between devices: 8.91 us -> 14.9 us  [on_device(): grad_row = lax.all_gather(gradient, 'role', axis=1, tiled=True)]
  transfers between devices with their start and end apart: 5 -> 7, of which waited for: 4 -> 6; matrix products, arithmetic and copies ran while one was open for 39% -> 42% of each run, Pallas kernels for 0% -> 0%
where the time goes in v1:
time: 402 us; the launch traced here: 394 us
  other arithmetic  125 us (31%)
  waiting for transfers between devices  111 us (28%)
  blocking collectives  91.1 us (23%)
  matrix products  24.2 us (6%)
  local copies, waits for them, and re-layouts  20.7 us (5%)
  between operations  17.7 us (4%)
  starting transfers between devices  4.17 us (1%)
    another operation x14, other arithmetic, on_device(): factor_lower = jnp.linalg.cholesky(gram_full)  78.7 us
    psum x1, blocking collectives, on_device(): lax.psum(jnp.sum(gradient_wide * gradient_wide), ('role', 'shard'))  44.2 us
    ppermute x3, waiting for transfers between devices, lower_gram(): lax.ppermute(tile_sums, 'shard', [(dev, dev ^ hop) for dev in range(8)])  42.2 us
    another operation x3, other arithmetic, on_device(): jax.scipy.linalg.solve_triangular(factor_lower, power_row.T, lower=True)  39.4 us
    psum x1, waiting for transfers between devices, on_device(): lax.psum((1.0 - smoothing) * squared * left_part + smoothing * placed, 'r...  33.9 us
    all_gather x1, blocking collectives, on_device(): lax.all_gather(basis_old, 'shard', axis=0, tiled=True).astype(jnp.float32)  32 us
    all_gather x1, waiting for transfers between devices, on_device(): lax.all_gather(gradient, 'shard', axis=0, tiled=True)  19.1 us
    all_gather x1, waiting for transfers between devices, on_device(): grad_row = lax.all_gather(gradient, 'role', axis=1, tiled=True)  14.9 us
  transfers between devices with their start and end apart: 7, of which 6 were waited for; matrix products, arithmetic and copies ran while one was open for 42% of the time, Pallas kernels for 0%

profile of v1, /device:TPU:0, one launch (start us, length us, event | category | flops | bytes accessed | tf_op | source)
XLA Modules:
  0.0 394.3 jit_solution(18165228630254049292)
XLA Ops:
  10.5 44.2 %psum.14 = f32[]{:T(128)} all-reduce(f32[]{:T(128)} %multiply_reduce_fusion), channel_id=1, replica_groups=mesh['role'=4,'shard'=8] {'role','shard'}, use_global_device_ids=true, to_apply=%region_1.0 | all-reduce | flops 1 | bytes 8 | tf_op jit(solution)/shard_map/psum | solution.py:67
  56.6 19.1 %all-gather.3.cloned.1.call-done = bf16[2560,640]{1,0:T(8,128)(2,1)} async-done(((bf16[320,640]{1,0:T(8,128)(2,1)}), bf16[2560,640]{1,0:T(8,128)(2,1)}) %all-gather.3.cloned.1.call-update) | async-done | bytes 3276816 | tf_op jit(solution)/shard_map/all_gather | solution.py:75
  75.7 5.3 %fusion = f32[320,2560]{1,0:T(8,128)} fusion(bf16[320,640]{1,0:T(8,128)(2,1)} %param.20, bf16[2560,640]{1,0:T(8,128)(2,1)} %all-gather.3.cloned.1.call-done, f32[320,2560]{1,0:T(8,128)S(1)} %constant_dynamic-update-slice_fusion.1, f32[]{:T(128)S(6)} %mul.51), kind=kOutput, calls=%fused_computation.3 | convolution fusion | flops 1051033600 | bytes 10240004 | tf_op jit(solution)/shard_map/dot_general | solution.py:73
  81.0 14.9 %all-gather.5.cloned.1.call-done = bf16[320,2560]{1,0:T(8,128)(2,1)} async-done(((bf16[320,640]{1,0:T(8,128)(2,1)}), bf16[320,2560]{1,0:T(8,128)(2,1)}) %all-gather.5.cloned.1.call-update) | async-done | bytes 1638416 | tf_op jit(solution)/shard_map/all_gather | solution.py:72
  96.0 6.3 %fusion.44 = f32[2560,640]{1,0:T(8,128)} fusion(bf16[320,2560]{1,0:T(8,128)(2,1)} %all-gather.5.cloned.1.call-done, bf16[320,640]{1,0:T(8,128)(2,1)S(1)} %copy-done), kind=kOutput, calls=%fused_computation.97 | convolution fusion | flops 1048576000 | bytes 8601600 | tf_op jit(solution)/shard_map/dot_general | solution.py:80
  103.1 32.0 %all_gather.17 = bf16[2560,128]{1,0:T(8,128)(2,1)S(1)} all-gather(bf16[320,128]{1,0:T(8,128)(2,1)S(1)} %copy-done.3), channel_id=1, replica_groups=mesh['role'=4,'shard'=8] {'shard'}, dimensions={0}, use_global_device_ids=true | all-gather | bytes 737280 | tf_op jit(solution)/shard_map/all_gather | solution.py:95
  135.1 33.9 %all-reduce.6.cloned.1.call-done = f32[320,2560]{1,0:T(8,128)} async-done(((f32[320,2560]{1,0:T(8,128)}), f32[320,2560]{1,0:T(8,128)}) %all-reduce.6.cloned.1.call-update) | async-done | bytes 3276816 | tf_op jit(solution)/shard_map/psum | solution.py:90
  169.0 3.5 fusion.45
  172.4 7.2 %all_gather.18 = f32[320,512]{1,0:T(8,128)S(1)} all-gather(f32[320,128]{1,0:T(8,128)S(1)} %fusion.45), channel_id=1, replica_groups=mesh['role'=4,'shard'=8] {'role'}, dimensions={1}, use_global_device_ids=true | all-gather | bytes 819200 | tf_op jit(solution)/shard_map/all_gather | solution.py:98
  182.5 8.9 %collective-permute-done = f32[64,576]{1,0:T(8,128)S(1)} collective-permute-done((f32[64,576]{1,0:T(8,128)S(1)}, f32[64,576]{1,0:T(8,128)S(1)}, u32[]{:S(2)}, u32[]{:S(2)}) %collective-permute-start) | collective-permute-done | bytes 147488 | tf_op jit(solution)/shard_map/ppermute | solution.py:41
  193.1 15.2 %collective-permute-done.1 = f32[64,576]{1,0:T(8,128)S(1)} collective-permute-done((f32[64,576]{1,0:T(8,128)S(1)}, f32[64,576]{1,0:T(8,128)S(1)}, u32[]{:S(2)}, u32[]{:S(2)}) %collective-permute-start.1) | collective-permute-done | bytes 147488 | tf_op jit(solution)/shard_map/ppermute | solution.py:41
  209.2 2.1 constant_dynamic-slice_fusion.1
  211.4 18.0 %collective-permute-done.2 = f32[64,576]{1,0:T(8,128)S(1)} collective-permute-done((f32[64,576]{1,0:T(8,128)S(1)}, f32[64,576]{1,0:T(8,128)S(1)}, u32[]{:S(2)}, u32[]{:S(2)}) %collective-permute-start.2) | collective-permute-done | bytes 147488 | tf_op jit(solution)/shard_map/ppermute | solution.py:41
  229.5 7.7 %all_gather.19 = f32[256,576]{1,0:T(8,128)S(1)} all-gather(f32[64,576]{1,0:T(8,128)S(1)} %add.129), channel_id=1, replica_groups=mesh['role'=4,'shard'=8] {'role'}, dimensions={0}, use_global_device_ids=true | all-gather | bytes 737280 | tf_op jit(solution)/shard_map/all_gather | solution.py:44
  247.5 11.7 %cholesky.103 = f32[128,128]{1,0:T(8,128)S(1)} custom-call(f32[128,128]{1,0:T(8,128)S(1)} %cholesky.263), custom_call_target="Cholesky" | custom-call | tf_op jit(solution)/shard_map/jit(cholesky)/cholesky | solution.py:100
  259.4 9.8 %custom-call.31 = f32[1,128,128]{1,2,0:T(8,128)S(1)} custom-call(f32[1,128,128]{2,1,0:T(8,128)S(1)} %get-tuple-element.126), custom_call_target="InvertDiagBlocksLowerTriangular" | custom-call | tf_op jit(solution)/shard_map/jit(cholesky)/cholesky | solution.py:100
  271.7 11.7 %cholesky.215 = f32[128,128]{1,0:T(8,128)S(1)} custom-call(f32[128,128]{1,0:T(8,128)S(1)} %cholesky.267), custom_call_target="Cholesky" | custom-call | tf_op jit(solution)/shard_map/jit(cholesky)/cholesky | solution.py:100
  283.5 10.0 %custom-call.32 = f32[1,128,128]{1,2,0:T(8,128)S(1)} custom-call(f32[1,128,128]{2,1,0:T(8,128)S(1)} %get-tuple-element.123), custom_call_target="InvertDiagBlocksLowerTriangular" | custom-call | tf_op jit(solution)/shard_map/jit(cholesky)/cholesky | solution.py:100
  295.0 11.7 %cholesky.236 = f32[128,128]{1,0:T(8,128)S(1)} custom-call(f32[128,128]{1,0:T(8,128)S(1)} %cholesky.272), custom_call_target="Cholesky" | custom-call | tf_op jit(solution)/shard_map/jit(cholesky)/cholesky | solution.py:100
  306.8 9.8 %custom-call.33 = f32[1,128,128]{1,2,0:T(8,128)S(1)} custom-call(f32[1,128,128]{2,1,0:T(8,128)S(1)} %get-tuple-element.120), custom_call_target="InvertDiagBlocksLowerTriangular" | custom-call | tf_op jit(solution)/shard_map/jit(cholesky)/cholesky | solution.py:100
  318.0 11.9 %cholesky.253 = f32[128,128]{1,0:T(8,128)S(1)} custom-call(f32[128,128]{1,0:T(8,128)S(1)} %convolution_subtract_fusion.5), custom_call_target="Cholesky" | custom-call | tf_op jit(solution)/shard_map/jit(cholesky)/cholesky | solution.py:100
  334.6 8.0 %while.9 = (s32[]{:T(128)}, f32[512,512]{1,0:T(8,128)S(1)}, s32[4,2]{0,1:T(2,128)S(1)}, f32[4,128,128]{2,1,0:T(8,128)S(1)}, s32[]{:T(128)}) while((s32[]{:T(128)}, f32[512,512]{1,0:T(8,128)S(1)}, s32[4,2]{0,1:T(2,128)S(1)}, f32[4,128,128]{2,1,0:T(8,128)S(1)}, s32[]{:T(128)}) %tuple.63), condition=%wide.while_cond.8, body=%wide.while_body.8.sunk | while | flops 2 | bytes 131181 | solution.py:101
  342.7 39.3 %custom-call.34 = f32[4,128,128]{1,2,0:T(8,128)S(1)} custom-call(f32[4,128,128]{2,1,0:T(8,128)S(1)} %get-tuple-element.106), custom_call_target="InvertDiagBlocksLowerTriangular" | custom-call | tf_op jit(solution)/shard_map/jit(_solve_triangular)/triangular_solve | solution.py:101
  385.2 2.4 multiply_add_fusion
  (89 shorter events, 40.0 us)
Async XLA Ops:
  7.2 68.5 %all-gather.3.cloned.1.call-start = ((), (), s32[]{:S(2)}) async-start(), calls=%async_computation.1 | async-start | bytes 3686400 | tf_op jit(solution)/shard_map/all_gather | solution.py:75
  7.9 88.1 %all-gather.5.cloned.1.call-start = ((), (), s32[]{:S(2)}) async-start(), calls=%async_computation.3 | async-start | bytes 2048000 | tf_op jit(solution)/shard_map/all_gather | solution.py:72
  8.6 160.3 %all-reduce.6.cloned.1.call-start = ((), (), s32[]{:S(2)}) async-start(), calls=%async_computation.2 | async-start | bytes 6553600 | tf_op jit(solution)/shard_map/psum | solution.py:90
  55.4 1.1 copy-start.2
  81.0 15.0 %copy-start = (bf16[320,640]{1,0:T(8,128)(2,1)S(1)}, bf16[320,640]{1,0:T(8,128)(2,1)}, u32[]{:S(2)}) copy-start(bf16[320,640]{1,0:T(8,128)(2,1)} %param.20) | copy-start | bytes 1228804
  81.0 304.2 %reduce-scatter.2.cloned.1.call-start = ((), (), s32[]{:S(2)}) async-start(), calls=%async_computation.4 | async-start | bytes 7372800 | tf_op jit(solution)/shard_map/reduce_scatter | solution.py:79
  102.2 0.9 copy-start.3
  181.0 10.5 %collective-permute-start = (f32[64,576]{1,0:T(8,128)S(1)}, f32[64,576]{1,0:T(8,128)S(1)}, u32[]{:S(2)}, u32[]{:S(2)}) collective-permute-start(f32[64,576]{1,0:T(8,128)S(1)} %fusion.16), channel_id=1, source_target_pairs={{0,1},{1,0},{2,3},{3,2},{4,5},{5,4},{6,7},{7,6},{8,9},{9,8},{10,11... | collective-permute-start | bytes 442376 | tf_op jit(solution)/shard_map/ppermute | solution.py:41
  191.5 16.8 %collective-permute-start.1 = (f32[64,576]{1,0:T(8,128)S(1)}, f32[64,576]{1,0:T(8,128)S(1)}, u32[]{:S(2)}, u32[]{:S(2)}) collective-permute-start(f32[64,576]{1,0:T(8,128)S(1)} %add.127), channel_id=1, source_target_pairs={{0,2},{1,3},{2,0},{3,1},{4,6},{5,7},{6,4},{7,5},{8,10},{9,11},{10,... | collective-permute-start | bytes 442376 | tf_op jit(solution)/shard_map/ppermute | solution.py:41
  208.3 21.1 %collective-permute-start.2 = (f32[64,576]{1,0:T(8,128)S(1)}, f32[64,576]{1,0:T(8,128)S(1)}, u32[]{:S(2)}, u32[]{:S(2)}) collective-permute-start(f32[64,576]{1,0:T(8,128)S(1)} %add.128), channel_id=1, source_target_pairs={{0,4},{1,5},{2,6},{3,7},{4,0},{5,1},{6,2},{7,3},{8,12},{9,13},{10,... | collective-permute-start | bytes 442376 | tf_op jit(solution)/shard_map/ppermute | solution.py:41
  246.5 1.0 copy-start.1
Sparse Core Ops, SparseCore 0:
  10.2 65.4 all-gather.2
  77.2 18.6 all-gather.4
  98.3 70.5 all-reduce.5
  172.4 132.0 reduce-scatter.1
